TPU v7x, 512 devices: a whole 4x8x8 slice. The times are simulated.
512 devices in a mesh: seq: 64 (over y, x, core), fsdp: 8 (over z).
Axes of the slice: x: 4, y: 8, z: 8, core: 2. Of those that a mesh axis runs over, the one named last changes fastest.
Arguments:
- activation_entries: bfloat16 [8192, 4096], P('seq', 'fsdp'), may hold values from -6 to 6
- content_mapping_matrix: bfloat16 [4096, 4096], P('seq', 'fsdp'), may hold values from -0.09375 to 0.09375
- content_lagged_blend: float32 [4096], P('fsdp'), may hold values from 0 to 1
- acceptance_vectors: bfloat16 [8192, 4096], P('seq', 'fsdp'), may hold values from -6 to 6
- address_vectors_given: bfloat16 [8192, 4096], P('seq', 'fsdp'), may hold values from -6 to 6
- inline_adaptation_speed: bfloat16 [8192, 4096], P('seq', 'fsdp'), may hold values from 0 to 1
- memory_fading_factors: float32 [8192, 4096], P('seq', 'fsdp'), may hold values from 0.6 to 1
- result_filter_given: bfloat16 [8192, 4096], P('seq', 'fsdp'), may hold values from 0.099609375 to 1.5
- extra_coordinate_factors: float32 [4096], P('fsdp'), may hold values from -0.75 to 0.75
- group_layernorm_scaling: float32 [4096], P('fsdp'), may hold values from 0.1 to 1.9
- group_layernorm_offset: float32 [4096], P('fsdp'), may hold values from -4 to 4
Outputs:
- time_mix: bfloat16 [8192, 4096], P('seq', 'fsdp')
All inputs are finite; a program needn't handle non-finite values.
Results may differ from a plain program's by a relative error of at most 0.0056.
Values may be sent and summed in bfloat16 or wider, within the bound.
A program may use at most 64 MiB of HBM per device.

v0:
```python
import jax
import jax.numpy as jnp
from jax import lax
from jax.sharding import PartitionSpec as P

GROUP_DIMENSION = 64
norm_eps = 0.00064
unit_eps = 1e-05
highest = lax.Precision.HIGHEST


def shifted_2(value, axis, steps):
    count = lax.axis_size(axis)
    first, last = (max(0, -steps), min(count, count - steps))
    return lax.ppermute(value, axis, [(source, source + steps) for source in range(first, last)])


def prefix_2(value, axis, join, neutral):
    count, mine = (lax.axis_size(axis), lax.axis_index(axis))
    pieces = lax.all_gather(value, axis)
    so_far = jnp.full_like(value, 0) + jnp.asarray(neutral, value.dtype)

    def step(position, so_far):
        longer = join(so_far, pieces[position])
        return jnp.where(position < mine, longer, so_far)

    return lax.fori_loop(0, count - 1, step, so_far)


def shards(
    activation_entries,
    content_mapping_matrix,
    content_lagged_blend,
    acceptance_vectors,
    address_vectors_given,
    inline_adaptation_speed,
    memory_fading_factors,
    result_filter_given,
    extra_coordinate_factors,
    group_layernorm_scaling,
    group_layernorm_offset,
):
    element_matrix_lines, portion_breadth = activation_entries.shape
    resident_groups = portion_breadth // GROUP_DIMENSION
    as_float = activation_entries.astype(jnp.float32)
    previous = shifted_2(activation_entries[-1:, :], "seq", 1)
    shifted = jnp.concatenate([previous.astype(jnp.float32), as_float[:-1]], axis=0)
    mixed = (as_float + (shifted - as_float) * content_lagged_blend[None, :]).astype(jnp.bfloat16)
    columns = lax.all_gather(content_mapping_matrix, "seq", axis=0, tiled=True)
    projected = jnp.dot(
        lax.all_gather(mixed, "fsdp", axis=1, tiled=True),
        columns,
        preferred_element_type=jnp.float32,
    )
    value = projected.astype(jnp.bfloat16)
    block_len = min(128, element_matrix_lines)
    blocks = element_matrix_lines // block_len

    def split_heads(array):
        shaped = array.astype(jnp.float32).reshape(
            blocks, block_len, resident_groups, GROUP_DIMENSION
        )
        return shaped.transpose(0, 2, 1, 3)

    rec_blocks = split_heads(acceptance_vectors)
    key_blocks = split_heads(address_vectors_given)
    rate_blocks = split_heads(inline_adaptation_speed)
    decay_blocks = split_heads(memory_fading_factors)
    value_blocks = split_heads(value)
    unit = key_blocks * lax.rsqrt(
        jnp.sum(key_blocks * key_blocks, axis=-1, keepdims=True) + unit_eps
    )
    cumul = jnp.cumprod(decay_blocks, axis=2)
    cumul_prev = jnp.concatenate([jnp.ones_like(cumul[:, :, :1]), cumul[:, :, :-1]], axis=2)
    cumul_end = cumul[:, :, -1:, :]
    erase_dir = -unit * cumul_prev
    write_dir = unit * rate_blocks / cumul
    key_scaled = key_blocks / cumul
    rec_scaled = rec_blocks * cumul
    strict = jnp.tril(jnp.ones((block_len, block_len), jnp.float32), -1)
    inclusive = jnp.tril(jnp.ones((block_len, block_len), jnp.float32))
    eye_block = jnp.eye(block_len, dtype=jnp.float32)
    erase_write = jnp.einsum("bhck,bhdk->bhcd", erase_dir, write_dir, precision=highest) * strict
    erase_key = jnp.einsum("bhck,bhdk->bhcd", erase_dir, key_scaled, precision=highest) * strict
    read_write = jnp.einsum("bhck,bhdk->bhcd", rec_scaled, write_dir, precision=highest) * inclusive
    read_key = jnp.einsum("bhck,bhdk->bhcd", rec_scaled, key_scaled, precision=highest) * inclusive
    system = eye_block - erase_write
    write_end = write_dir * cumul_end
    key_end = key_scaled * cumul_end

    def run_blocks(initial, values, want_rows):

        def block_step(state, inputs):
            (
                erase_b,
                rec_b,
                system_b,
                erase_key_b,
                read_write_b,
                read_key_b,
                write_e,
                key_e,
                cumul_e,
                value_b,
            ) = inputs
            rhs = jnp.einsum("hck,hrk->hcr", erase_b, state, precision=highest) + jnp.einsum(
                "hcd,hdr->hcr", erase_key_b, value_b, precision=highest
            )
            pseudo = lax.linalg.triangular_solve(
                system_b, rhs, left_side=True, lower=True, unit_diagonal=True
            )
            new_state = (
                state * cumul_e
                + jnp.einsum("hcr,hck->hrk", pseudo, write_e, precision=highest)
                + jnp.einsum("hcr,hck->hrk", value_b, key_e, precision=highest)
            )
            if want_rows:
                out_rows = (
                    jnp.einsum("hck,hrk->hcr", rec_b, state, precision=highest)
                    + jnp.einsum("hcd,hdr->hcr", read_write_b, pseudo, precision=highest)
                    + jnp.einsum("hcd,hdr->hcr", read_key_b, value_b, precision=highest)
                )
                return (new_state, out_rows)
            return (new_state, None)

        inputs = (
            erase_dir,
            rec_scaled,
            system,
            erase_key,
            read_write,
            read_key,
            write_end,
            key_end,
            cumul_end,
            values,
        )
        return lax.scan(block_step, initial, inputs)

    identity_part = jnp.broadcast_to(
        jnp.eye(GROUP_DIMENSION, dtype=jnp.float32),
        (resident_groups, GROUP_DIMENSION, GROUP_DIMENSION),
    )
    zero_part = jnp.zeros((resident_groups, GROUP_DIMENSION, GROUP_DIMENSION), jnp.float32)
    start_aug = jnp.concatenate([zero_part, identity_part], axis=1)
    values_aug = jnp.concatenate([value_blocks, jnp.zeros_like(value_blocks)], axis=-1)
    ends, outs_aug = run_blocks(start_aug, values_aug, False)
    payload = jnp.swapaxes(ends, 1, 2)

    def combine_pairs(earlier, later):
        moved = jnp.einsum(
            "hij,hjr->hir", later[:, :, GROUP_DIMENSION:], earlier, precision=highest
        )
        return moved + jnp.concatenate(
            [later[:, :, :GROUP_DIMENSION], jnp.zeros_like(later[:, :, GROUP_DIMENSION:])], axis=-1
        )

    identity_pair = jnp.concatenate([zero_part, identity_part], axis=-1)
    prefix = prefix_2(payload, "seq", combine_pairs, identity_pair)
    incoming = jnp.swapaxes(prefix[:, :, :GROUP_DIMENSION], 1, 2)
    final_state, read_blocks = run_blocks(incoming, value_blocks, True)
    read = read_blocks.transpose(0, 2, 1, 3).reshape(
        element_matrix_lines, resident_groups, GROUP_DIMENSION
    )
    centre = read - jnp.mean(read, axis=-1, keepdims=True)
    spread = jnp.mean(centre * centre, axis=-1, keepdims=True)
    standardized_result = (centre * lax.rsqrt(spread + norm_eps)).reshape(
        element_matrix_lines, portion_breadth
    ) * group_layernorm_scaling[None, :] + group_layernorm_offset[None, :]
    acceptance_by_group = acceptance_vectors.astype(jnp.float32).reshape(
        element_matrix_lines, resident_groups, GROUP_DIMENSION
    )
    address_by_group = address_vectors_given.astype(jnp.float32).reshape(
        element_matrix_lines, resident_groups, GROUP_DIMENSION
    )
    content_by_group = value.astype(jnp.float32).reshape(
        element_matrix_lines, resident_groups, GROUP_DIMENSION
    )
    scaled_aggregate_figure = jnp.sum(
        acceptance_by_group
        * address_by_group
        * extra_coordinate_factors.reshape(resident_groups, GROUP_DIMENSION)[None],
        axis=-1,
        keepdims=True,
    )
    present_extra_term = (scaled_aggregate_figure * content_by_group).reshape(
        element_matrix_lines, portion_breadth
    )
    return (
        (standardized_result + present_extra_term) * result_filter_given.astype(jnp.float32)
    ).astype(jnp.bfloat16)


def solution(mesh):
    return jax.shard_map(
        shards,
        mesh=mesh,
        in_specs=(
            P("seq", "fsdp"),
            P("seq", "fsdp"),
            P("fsdp"),
            P("seq", "fsdp"),
            P("seq", "fsdp"),
            P("seq", "fsdp"),
            P("seq", "fsdp"),
            P("seq", "fsdp"),
            P("fsdp"),
            P("fsdp"),
            P("fsdp"),
        ),
        out_specs=P("seq", "fsdp"),
        check_vma=False,
    )
```

profile of v0, /device:TPU:1, one launch (start us, length us, event | category | flops | bytes accessed | tf_op | source)
XLA Modules:
  0.0 370.4 jit_solution(16223546304854679737)
XLA Ops:
  7.2 4.5 %collective-permute-start = (bf16[1,512]{1,0:T(2,128)(2,1)S(1)}, bf16[1,512]{1,0:T(2,128)(2,1)S(1)}, u32[]{:S(2)}, u32[]{:S(2)}) collective-permute-start(bf16[1,512]{1,0:T(2,128)(2,1)S(1)} %slice.40), channel_id=1, source_target_pairs={{0,8},{8,16},{16,24},{24,32},{32,40},{40,48},{48,56},{56,64},{64,7... | collective-permute-start | bytes 3080 | tf_op jit(solution)/shard_map/ppermute | solution.py:15
  12.7 3.4 collective-permute-done
  16.0 1.6 fusion.25
  18.5 1.0 copy.54
  19.5 1.1 copy.50
  20.6 1.1 copy.52
  22.0 1.0 copy.56
  23.4 23.3 %fusion.43 = f32[1,8,128,64]{3,1,2,0:T(8,128)S(1)} fusion(f32[1,8,128,64]{3,1,2,0:T(8,128)S(1)} %copy.53), kind=kOutput, calls=%fused_computation.81 | output fusion | flops 8323072 | bytes 524288 | tf_op jit(solution)/shard_map/jit(cumprod)/reduce_window | solution.py:73
  48.0 2.7 multiply_bitcast_fusion.1
  50.7 1.2 copy.58
  51.9 1.2 copy.62
  53.1 1.2 copy.59
  54.6 1.0 fusion.6
  55.6 79.2 %custom-call.7 = f32[8,1,128,128]{2,3,1,0:T(8,128)} custom-call(f32[8,1,128,128]{3,2,1,0:T(8,128)S(1)} %fusion.6), custom_call_target="InvertDiagBlocksLowerTriangular" | custom-call | tf_op jit(solution)/shard_map/while/body/eval_jaxpr/triangular_solve | solution.py:109
  135.5 1.9 fusion.21
  137.4 1.0 convolution_multiply_fusion.2
  138.5 10.8 %all-gather.7.cloned.1.call-done = bf16[4096,512]{1,0:T(8,128)(2,1)} async-done(((bf16[64,512]{1,0:T(8,128)(2,1)}), bf16[4096,512]{1,0:T(8,128)(2,1)}) %all-gather.7.cloned.1.call-update) | async-done | bytes 4194320 | tf_op jit(solution)/shard_map/all_gather | solution.py:49
  149.3 3.2 convolution_convert_fusion
  153.4 1.1 copy.64
  154.5 1.7 convolution_add_fusion.1
  156.2 2.1 fusion.12
  158.3 1.1 convolution_add_fusion.6
  159.4 1.7 fusion.7
  163.9 1.2 copy.70
  165.3 1.0 convolution_multiply_fusion.1
  166.3 1.0 convolution_multiply_fusion
  168.1 96.3 %all-gather.9.cloned.1.call-done = f32[512,64,128]{2,1,0:T(8,128)} async-done(((f32[8,64,128]{2,1,0:T(8,128)}), f32[512,64,128]{2,1,0:T(8,128)}) %all-gather.9.cloned.1.call-update) | async-done | bytes 16777232 | tf_op jit(solution)/shard_map/all_gather | solution.py:20
  264.3 93.2 %while.8 = (s32[]{:T(128)}, f32[8,64,128]{2,1,0:T(8,128)S(1)}, s32[]{:T(128)}, f32[64,8,64,128]{3,2,1,0:T(8,128)}, s32[]{:T(128)}, /*index=5*/pred[128]{0:T(512)(128)(4,1)S(1)}) while((s32[]{:T(128)}, f32[8,64,128]{2,1,0:T(8,128)S(1)}, s32[]{:T(128)}, f32[64,8,64,128]{3,2,1,0:T(8,128)}, s32[]{:T(128)}, ...), condition=%wide.region_3.4_spmd, body=%wide.region_2.3_spmd.sunk | while | flops 50528256 | bytes 2359899 | solution.py:27
  264.4 1.0 dynamic-slice_bitcast_fusion.2
  265.9 1.0 dynamic-slice_bitcast_fusion.2
  267.4 1.0 dynamic-slice_bitcast_fusion.2
  268.9 1.0 dynamic-slice_bitcast_fusion.2
  271.8 1.0 dynamic-slice_bitcast_fusion.2
  273.3 1.0 dynamic-slice_bitcast_fusion.2
  274.8 1.0 dynamic-slice_bitcast_fusion.2
  276.2 1.0 dynamic-slice_bitcast_fusion.2
  277.7 1.0 dynamic-slice_bitcast_fusion.2
  279.2 1.0 dynamic-slice_bitcast_fusion.2
  282.2 1.0 dynamic-slice_bitcast_fusion.2
  285.1 1.0 dynamic-slice_bitcast_fusion.2
  286.6 1.0 dynamic-slice_bitcast_fusion.2
  288.1 1.0 dynamic-slice_bitcast_fusion.2
  289.6 1.0 dynamic-slice_bitcast_fusion.2
  291.0 1.0 dynamic-slice_bitcast_fusion.2
  292.5 1.0 dynamic-slice_bitcast_fusion.2
  295.5 1.0 dynamic-slice_bitcast_fusion.2
  297.0 1.0 dynamic-slice_bitcast_fusion.2
  298.4 1.0 dynamic-slice_bitcast_fusion.2
  299.9 1.0 dynamic-slice_bitcast_fusion.2
  301.4 1.0 dynamic-slice_bitcast_fusion.2
  302.9 1.0 dynamic-slice_bitcast_fusion.2
  304.3 1.0 dynamic-slice_bitcast_fusion.2
  305.8 1.0 dynamic-slice_bitcast_fusion.2
  308.8 1.0 dynamic-slice_bitcast_fusion.2
  310.3 1.0 dynamic-slice_bitcast_fusion.2
  311.7 1.0 dynamic-slice_bitcast_fusion.2
  313.2 1.0 dynamic-slice_bitcast_fusion.2
  314.7 1.0 dynamic-slice_bitcast_fusion.2
  316.2 1.0 dynamic-slice_bitcast_fusion.2
  319.1 1.0 dynamic-slice_bitcast_fusion.2
  320.6 1.0 dynamic-slice_bitcast_fusion.2
  322.1 1.0 dynamic-slice_bitcast_fusion.2
  358.6 1.6 convolution_add_fusion.4
  360.8 1.1 convolution_add_fusion.3
  (229 shorter events, 70.7 us)
Async XLA Ops:
  6.5 131.9 %all-gather.5.cloned.1.call-start = ((), (), s32[]{:S(2)}) async-start(), calls=%async_computation | async-start | bytes 1179648 | tf_op jit(solution)/shard_map/all_gather | solution.py:51
  7.2 8.8 %collective-permute-start = (bf16[1,512]{1,0:T(2,128)(2,1)S(1)}, bf16[1,512]{1,0:T(2,128)(2,1)S(1)}, u32[]{:S(2)}, u32[]{:S(2)}) collective-permute-start(bf16[1,512]{1,0:T(2,128)(2,1)S(1)} %slice.40), channel_id=1, source_target_pairs={{0,8},{8,16},{16,24},{24,32},{32,40},{40,48},{48,56},{56,64},{64,7... | collective-permute-start | bytes 3080 | tf_op jit(solution)/shard_map/ppermute | solution.py:15
  17.7 131.6 %all-gather.7.cloned.1.call-start = ((), (), s32[]{:S(2)}) async-start(), calls=%async_computation.1 | async-start | bytes 4259840 | tf_op jit(solution)/shard_map/all_gather | solution.py:49
  18.5 245.9 %all-gather.9.cloned.1.call-start = ((), (), s32[]{:S(2)}) async-start(), calls=%async_computation.2 | async-start | bytes 17039360 | tf_op jit(solution)/shard_map/all_gather | solution.py:20
  19.5 31.2 %copy-start.2 = (bf16[128,512]{0,1:T(8,128)(2,1)}, bf16[128,512]{0,1:T(8,128)(2,1)S(1)}, u32[]{:S(2)}) copy-start(bf16[128,512]{0,1:T(8,128)(2,1)S(1)} %copy.54) | copy-start | bytes 393220
  20.6 30.1 %copy-start.4 = (bf16[128,512]{0,1:T(8,128)(2,1)}, bf16[128,512]{0,1:T(8,128)(2,1)S(1)}, u32[]{:S(2)}) copy-start(bf16[128,512]{0,1:T(8,128)(2,1)S(1)} %copy.50) | copy-start | bytes 393220
  134.8 0.6 copy-start.7
  152.5 9.4 %copy-start.12 = (f32[512]{0:T(512)S(1)}, f32[512]{0:T(512)}, u32[]{:S(2)}) copy-start(f32[512]{0:T(512)} %param.21) | copy-start | bytes 6148
  152.5 9.5 %copy-start.3 = (bf16[128,512]{0,1:T(8,128)(2,1)S(1)}, bf16[128,512]{0,1:T(8,128)(2,1)}, u32[]{:S(2)}) copy-start(bf16[128,512]{0,1:T(8,128)(2,1)} %copy-done.2) | copy-start | bytes 393220
  152.5 9.5 %copy-start.5 = (bf16[128,512]{0,1:T(8,128)(2,1)S(1)}, bf16[128,512]{0,1:T(8,128)(2,1)}, u32[]{:S(2)}) copy-start(bf16[128,512]{0,1:T(8,128)(2,1)} %copy-done.4) | copy-start | bytes 393220
  159.4 105.0 %copy-start.9 = (pred[128]{0:T(512)(128)(4,1)S(1)}, pred[128]{0:T(512)(128)(4,1)}, u32[]{:S(2)}) copy-start(pred[128]{0:T(512)(128)(4,1)} %constant.95.clone.1) | copy-start | bytes 388
  264.3 95.8 %copy-start = (f32[8,1,128,128]{2,3,1,0:T(8,128)S(1)}, f32[8,1,128,128]{2,3,1,0:T(8,128)}, u32[]{:S(2)}) copy-start(f32[8,1,128,128]{2,3,1,0:T(8,128)} %custom-call.7) | copy-start | bytes 1572868
  357.8 4.1 %copy-start.1 = (bf16[128,512]{0,1:T(8,128)(2,1)S(1)}, bf16[128,512]{0,1:T(8,128)(2,1)}, u32[]{:S(2)}) copy-start(bf16[128,512]{0,1:T(8,128)(2,1)} %copy.74) | copy-start | bytes 393220
  357.8 5.3 %copy-start.10 = (f32[512]{0:T(512)S(1)}, f32[512]{0:T(512)}, u32[]{:S(2)}) copy-start(f32[512]{0:T(512)} %param.23) | copy-start | bytes 6148
  357.8 5.3 %copy-start.11 = (f32[512]{0:T(512)S(1)}, f32[512]{0:T(512)}, u32[]{:S(2)}) copy-start(f32[512]{0:T(512)} %param.22) | copy-start | bytes 6148
  358.5 4.6 %copy-start.6 = (f32[128,512]{1,0:T(8,128)S(1)}, f32[128,512]{1,0:T(8,128)}, u32[]{:S(2)}) copy-start(f32[128,512]{1,0:T(8,128)} %copy.81) | copy-start | bytes 786436
  360.2 2.9 copy-start.8
Sparse Core Ops, SparseCore 0:
  17.8 40.1 all-gather.4
  61.4 87.8 all-gather.6
  161.2 103.0 all-gather.8
where the time goes:
time: 373 us; the launch traced here: 370 us
  waiting for transfers between devices  111 us (30%)
  other arithmetic  109 us (29%)
  local copies, waits for them, and re-layouts  81 us (22%)
  matrix products  48.5 us (13%)
  between operations  13.7 us (4%)
  starting transfers between devices  4.58 us (1%)
    all_gather x1, waiting for transfers between devices, prefix_2(): pieces = lax.all_gather(value, axis)  96.3 us
    another operation x4, other arithmetic, block_step(): lax.linalg.triangular_solve(system_b, rhs, left_side=True, lower=True, un...  79.3 us
    squeeze x63, local copies, waits for them, and re-layouts, step(): longer = join(so_far, pieces[position])  61.5 us
    dot_general x63, matrix products, combine_pairs(): jnp.einsum('hij,hjr->hir', later[:, :, GROUP_DIMENSION:], earlier, precis...  28.1 us
    another operation x1, other arithmetic, shards(): cumul = jnp.cumprod(decay_blocks, axis=2)  23.3 us
    all_gather x1, waiting for transfers between devices, shards(): columns = lax.all_gather(content_mapping_matrix, 'seq', axis=0, tiled=True)  10.8 us
  transfers between devices with their start and end apart: 4, of which 3 were waited for; matrix products, arithmetic and copies ran while one was open for 34% of the time, Pallas kernels for 0%

commit v1 on v0

--- a/solution.py
+++ b/solution.py
@@ -1,3 +1,4 @@
+import functools
 import jax
 import jax.numpy as jnp
 from jax import lax
@@ -7,6 +8,16 @@
 norm_eps = 0.00064
 unit_eps = 1e-05
 highest = lax.Precision.HIGHEST
+
+
+def bring_the_task(v0, mesh_ax):
+    opened = jnp.concatenate(
+        lax.all_to_all(jnp.stack(lax.axis_size(mesh_ax) * [v0]), mesh_ax, 0, 0), axis=0
+    )
+    return opened
+
+
+push_the_spots = functools.partial(bring_the_task, mesh_ax="seq")
 
 
 def shifted_2(value, axis, steps):
@@ -46,7 +57,7 @@
     previous = shifted_2(activation_entries[-1:, :], "seq", 1)
     shifted = jnp.concatenate([previous.astype(jnp.float32), as_float[:-1]], axis=0)
     mixed = (as_float + (shifted - as_float) * content_lagged_blend[None, :]).astype(jnp.bfloat16)
-    columns = lax.all_gather(content_mapping_matrix, "seq", axis=0, tiled=True)
+    columns = push_the_spots(content_mapping_matrix)
     projected = jnp.dot(
         lax.all_gather(mixed, "fsdp", axis=1, tiled=True),
         columns,

time: 373 us -> 434 us (1.16)
  waiting for transfers between devices: 111 us -> 163 us
  starting transfers between devices: 4.58 us -> 15.8 us
    all_gather x1, waiting for transfers between devices: 96.3 us -> 153 us  [prefix_2(): pieces = lax.all_gather(value, axis)]
    all_to_all x0 -> x1, starting transfers between devices: none -> 12 us  [bring_the_task(): lax.all_to_all(jnp.stack(lax.axis_size(mesh_ax) * [v0]), mesh_ax, 0, 0)]
    all_gather x1 -> x0, waiting for transfers between devices: 10.8 us -> none  [shards(): columns = lax.all_gather(content_mapping_matrix, 'seq', axis=0, tiled=True)]
    all_gather x1, waiting for transfers between devices: 0.02 us -> 9.86 us  [shards(): lax.all_gather(mixed, 'fsdp', axis=1, tiled=True)]
  transfers between devices with their start and end apart: 4 -> 4, of which waited for: 3 -> 2; matrix products, arithmetic and copies ran while one was open for 34% -> 29% of each run, Pallas kernels for 0% -> 0%
where the time goes in v1:
time: 434 us; the launch traced here: 431 us
  waiting for transfers between devices  163 us (38%)
  other arithmetic  108 us (25%)
  local copies, waits for them, and re-layouts  79 us (18%)
  matrix products  48.5 us (11%)
  starting transfers between devices  15.8 us (4%)
  between operations  14.1 us (3%)
    all_gather x1, waiting for transfers between devices, prefix_2(): pieces = lax.all_gather(value, axis)  153 us
    another operation x4, other arithmetic, block_step(): lax.linalg.triangular_solve(system_b, rhs, left_side=True, lower=True, un...  79.5 us
    squeeze x63, local copies, waits for them, and re-layouts, step(): longer = join(so_far, pieces[position])  61.5 us
    dot_general x63, matrix products, combine_pairs(): jnp.einsum('hij,hjr->hir', later[:, :, GROUP_DIMENSION:], earlier, precis...  28.1 us
    another operation x1, other arithmetic, shards(): cumul = jnp.cumprod(decay_blocks, axis=2)  23.3 us
    all_to_all x1, starting transfers between devices, bring_the_task(): lax.all_to_all(jnp.stack(lax.axis_size(mesh_ax) * [v0]), mesh_ax, 0, 0)  12 us
    all_gather x1, waiting for transfers between devices, shards(): lax.all_gather(mixed, 'fsdp', axis=1, tiled=True)  9.86 us
  transfers between devices with their start and end apart: 4, of which 2 were waited for; matrix products, arithmetic and copies ran while one was open for 29% of the time, Pallas kernels for 0%

profile of v1, /device:TPU:1, one launch (start us, length us, event | category | flops | bytes accessed | tf_op | source)
XLA Modules:
  0.0 431.1 jit_solution(1245224375036654320)
XLA Ops:
  6.5 3.3 stack.2
  9.9 12.0 %all-to-all-start = ((bf16[64,64,512]{2,1,0:T(8,128)(2,1)}), bf16[64,64,512]{2,1,0:T(8,128)(2,1)}, u32[]{:S(2)}, u32[]{:S(2)}) async-start(bf16[64,64,512]{2,1,0:T(8,128)(2,1)} %stack.2), calls=%async_computation | async-start | bytes 8388608 | tf_op jit(solution)/shard_map/all_to_all | solution.py:15
  22.0 3.7 collective-permute-start
  26.7 23.3 %fusion.43 = f32[1,8,128,64]{3,1,2,0:T(8,128)S(1)} fusion(f32[1,8,128,64]{3,1,2,0:T(8,128)S(1)} %copy.53), kind=kOutput, calls=%fused_computation.81 | output fusion | flops 8323072 | bytes 524288 | tf_op jit(solution)/shard_map/jit(cumprod)/reduce_window | solution.py:84
  52.4 2.6 multiply_bitcast_fusion.1
  55.0 1.2 copy.58
  56.2 1.2 copy.62
  57.5 1.2 copy.59
  58.9 1.0 fusion.6
  59.9 79.4 %custom-call.7 = f32[8,1,128,128]{2,3,1,0:T(8,128)} custom-call(f32[8,1,128,128]{3,2,1,0:T(8,128)S(1)} %fusion.6), custom_call_target="InvertDiagBlocksLowerTriangular" | custom-call | tf_op jit(solution)/shard_map/while/body/eval_jaxpr/triangular_solve | solution.py:120
  140.0 1.9 fusion.21
  141.9 1.0 convolution_multiply_fusion.2
  142.9 9.9 %all-gather.4.cloned.1.call-done = bf16[128,4096]{1,0:T(8,128)(2,1)} async-done(((bf16[128,512]{1,0:T(8,128)(2,1)}), bf16[128,4096]{1,0:T(8,128)(2,1)}) %all-gather.4.cloned.1.call-update) | async-done | bytes 1048592 | tf_op jit(solution)/shard_map/all_gather | solution.py:62
  152.8 3.2 convolution_convert_fusion
  156.8 1.1 copy.64
  158.0 1.7 convolution_add_fusion.1
  159.7 2.1 fusion.12
  161.7 1.1 convolution_add_fusion.6
  162.8 1.7 fusion.7
  167.1 1.2 copy.70
  168.6 1.0 convolution_multiply_fusion.1
  169.6 1.0 convolution_multiply_fusion
  171.3 153.1 %all-gather.6.cloned.1.call-done = f32[512,64,128]{2,1,0:T(8,128)} async-done(((f32[8,64,128]{2,1,0:T(8,128)}), f32[512,64,128]{2,1,0:T(8,128)}) %all-gather.6.cloned.1.call-update) | async-done | bytes 16777232 | tf_op jit(solution)/shard_map/all_gather | solution.py:31
  324.5 93.4 %while.8 = (s32[]{:T(128)}, f32[8,64,128]{2,1,0:T(8,128)S(1)}, s32[]{:T(128)}, f32[64,8,64,128]{3,2,1,0:T(8,128)}, s32[]{:T(128)}, /*index=5*/pred[128]{0:T(512)(128)(4,1)S(1)}) while((s32[]{:T(128)}, f32[8,64,128]{2,1,0:T(8,128)S(1)}, s32[]{:T(128)}, f32[64,8,64,128]{3,2,1,0:T(8,128)}, s32[]{:T(128)}, ...), condition=%wide.region_3.4_spmd, body=%wide.region_2.3_spmd.sunk | while | flops 50528256 | bytes 2359899 | solution.py:38
  324.5 1.0 dynamic-slice_bitcast_fusion.2
  326.0 1.0 dynamic-slice_bitcast_fusion.2
  327.5 1.0 dynamic-slice_bitcast_fusion.2
  330.4 1.0 dynamic-slice_bitcast_fusion.2
  331.9 1.0 dynamic-slice_bitcast_fusion.2
  333.4 1.0 dynamic-slice_bitcast_fusion.2
  334.9 1.0 dynamic-slice_bitcast_fusion.2
  336.4 1.0 dynamic-slice_bitcast_fusion.2
  337.8 1.0 dynamic-slice_bitcast_fusion.2
  339.3 1.0 dynamic-slice_bitcast_fusion.2
  343.8 1.0 dynamic-slice_bitcast_fusion.2
  345.2 1.0 dynamic-slice_bitcast_fusion.2
  346.7 1.0 dynamic-slice_bitcast_fusion.2
  348.2 1.0 dynamic-slice_bitcast_fusion.2
  349.7 1.0 dynamic-slice_bitcast_fusion.2
  351.1 1.0 dynamic-slice_bitcast_fusion.2
  355.6 1.0 dynamic-slice_bitcast_fusion.2
  357.1 1.0 dynamic-slice_bitcast_fusion.2
  358.5 1.0 dynamic-slice_bitcast_fusion.2
  360.0 1.0 dynamic-slice_bitcast_fusion.2
  361.5 1.0 dynamic-slice_bitcast_fusion.2
  363.0 1.0 dynamic-slice_bitcast_fusion.2
  364.5 1.0 dynamic-slice_bitcast_fusion.2
  367.4 1.0 dynamic-slice_bitcast_fusion.2
  368.9 1.0 dynamic-slice_bitcast_fusion.2
  370.4 1.0 dynamic-slice_bitcast_fusion.2
  371.8 1.0 dynamic-slice_bitcast_fusion.2
  373.3 1.0 dynamic-slice_bitcast_fusion.2
  374.8 1.0 dynamic-slice_bitcast_fusion.2
  376.3 1.0 dynamic-slice_bitcast_fusion.2
  380.7 1.0 dynamic-slice_bitcast_fusion.2
  382.2 1.0 dynamic-slice_bitcast_fusion.2
  383.7 1.0 dynamic-slice_bitcast_fusion.2
  385.2 1.0 dynamic-slice_bitcast_fusion.2
  386.6 1.0 dynamic-slice_bitcast_fusion.2
  388.1 1.0 dynamic-slice_bitcast_fusion.2
  392.6 1.0 dynamic-slice_bitcast_fusion.2
  394.0 1.0 dynamic-slice_bitcast_fusion.2
  418.9 1.6 convolution_add_fusion.4
  421.1 1.1 convolution_add_fusion.3
  (241 shorter events, 65.5 us)
Async XLA Ops:
  9.9 12.1 %copy-start.1 = (bf16[128,512]{1,0:T(8,128)(2,1)S(1)}, bf16[128,512]{1,0:T(8,128)(2,1)}, u32[]{:S(2)}) copy-start(bf16[128,512]{1,0:T(8,128)(2,1)} %param.13) | copy-start | bytes 393220
  9.9 15.8 %copy-start.10 = (bf16[128,512]{1,0:T(8,128)(2,1)S(1)}, bf16[128,512]{1,0:T(8,128)(2,1)}, u32[]{:S(2)}) copy-start(bf16[128,512]{1,0:T(8,128)(2,1)} %param.17) | copy-start | bytes 393220
  9.9 16.0 %copy-start.9 = (f32[128,512]{1,0:T(8,128)S(1)}, f32[128,512]{1,0:T(8,128)}, u32[]{:S(2)}) copy-start(f32[128,512]{1,0:T(8,128)} %param.19) | copy-start | bytes 786436
  9.9 142.9 %all-to-all-start = ((bf16[64,64,512]{2,1,0:T(8,128)(2,1)}), bf16[64,64,512]{2,1,0:T(8,128)(2,1)}, u32[]{:S(2)}, u32[]{:S(2)}) async-start(bf16[64,64,512]{2,1,0:T(8,128)(2,1)} %stack.2), calls=%async_computation | async-start | bytes 8388608 | tf_op jit(solution)/shard_map/all_to_all | solution.py:15
  21.9 28.2 %copy-start.15 = (f32[512]{0:T(512)S(1)}, f32[512]{0:T(512)}, u32[]{:S(2)}) copy-start(f32[512]{0:T(512)} %param.15) | copy-start | bytes 6148
  21.9 29.8 %copy-start.11 = (bf16[128,512]{1,0:T(8,128)(2,1)S(1)}, bf16[128,512]{1,0:T(8,128)(2,1)}, u32[]{:S(2)}) copy-start(bf16[128,512]{1,0:T(8,128)(2,1)} %param.16) | copy-start | bytes 393220
  21.9 29.9 %copy-start.12 = (bf16[128,512]{1,0:T(8,128)(2,1)S(1)}, bf16[128,512]{1,0:T(8,128)(2,1)}, u32[]{:S(2)}) copy-start(bf16[128,512]{1,0:T(8,128)(2,1)} %param.18) | copy-start | bytes 393220
  21.9 130.8 %all-gather.4.cloned.1.call-start = ((), (), s32[]{:S(2)}) async-start(), calls=%async_computation.1 | async-start | bytes 1179648 | tf_op jit(solution)/shard_map/all_gather | solution.py:62
  22.0 28.1 %collective-permute-start = (bf16[1,512]{1,0:T(2,128)(2,1)S(1)}, bf16[1,512]{1,0:T(2,128)(2,1)S(1)}, u32[]{:S(2)}, u32[]{:S(2)}) collective-permute-start(bf16[1,512]{1,0:T(2,128)(2,1)S(1)} %slice.40), channel_id=1, source_target_pairs={{0,8},{8,16},{16,24},{24,32},{32,40},{40,48},{48,56},{56,64},{64,7... | collective-permute-start | bytes 3080 | tf_op jit(solution)/shard_map/ppermute | solution.py:26
  25.8 0.7 copy-start.3
  50.9 273.6 %all-gather.6.cloned.1.call-start = ((), (), s32[]{:S(2)}) async-start(), calls=%async_computation.2 | async-start | bytes 17039360 | tf_op jit(solution)/shard_map/all_gather | solution.py:31
  51.9 5.6 %copy-start.5 = (bf16[128,512]{0,1:T(8,128)(2,1)}, bf16[128,512]{0,1:T(8,128)(2,1)S(1)}, u32[]{:S(2)}) copy-start(bf16[128,512]{0,1:T(8,128)(2,1)S(1)} %copy.50) | copy-start | bytes 393220
  139.4 0.6 copy-start.8
  156.0 9.4 %copy-start.18 = (f32[512]{0:T(512)S(1)}, f32[512]{0:T(512)}, u32[]{:S(2)}) copy-start(f32[512]{0:T(512)} %param.21) | copy-start | bytes 6148
  156.0 9.5 %copy-start.4 = (bf16[128,512]{0,1:T(8,128)(2,1)S(1)}, bf16[128,512]{0,1:T(8,128)(2,1)}, u32[]{:S(2)}) copy-start(bf16[128,512]{0,1:T(8,128)(2,1)} %copy-done.3) | copy-start | bytes 393220
  156.0 9.5 %copy-start.6 = (bf16[128,512]{0,1:T(8,128)(2,1)S(1)}, bf16[128,512]{0,1:T(8,128)(2,1)}, u32[]{:S(2)}) copy-start(bf16[128,512]{0,1:T(8,128)(2,1)} %copy-done.5) | copy-start | bytes 393220
  162.8 161.6 %copy-start.14 = (pred[128]{0:T(512)(128)(4,1)S(1)}, pred[128]{0:T(512)(128)(4,1)}, u32[]{:S(2)}) copy-start(pred[128]{0:T(512)(128)(4,1)} %constant.95.clone.1) | copy-start | bytes 388
  324.5 96.0 %copy-start = (f32[8,1,128,128]{2,3,1,0:T(8,128)S(1)}, f32[8,1,128,128]{2,3,1,0:T(8,128)}, u32[]{:S(2)}) copy-start(f32[8,1,128,128]{2,3,1,0:T(8,128)} %custom-call.7) | copy-start | bytes 1572868
  418.1 4.1 copy-start.2
  418.1 5.3 %copy-start.16 = (f32[512]{0:T(512)S(1)}, f32[512]{0:T(512)}, u32[]{:S(2)}) copy-start(f32[512]{0:T(512)} %param.23) | copy-start | bytes 6148
  418.1 5.3 %copy-start.17 = (f32[512]{0:T(512)S(1)}, f32[512]{0:T(512)}, u32[]{:S(2)}) copy-start(f32[512]{0:T(512)} %param.22) | copy-start | bytes 6148
  418.9 4.6 %copy-start.7 = (f32[128,512]{1,0:T(8,128)S(1)}, f32[128,512]{1,0:T(8,128)}, u32[]{:S(2)}) copy-start(f32[128,512]{1,0:T(8,128)} %copy.81) | copy-start | bytes 786436
  420.5 3.0 copy-start.13
Sparse Core Ops, SparseCore 0:
  51.0 101.7 all-gather.3
  164.7 159.7 all-gather.5
